TPU v7x, 32 devices: a whole 2x2x4 slice. The times are simulated.
32 devices in a mesh: src: 4 (over x, core), rcv: 8 (over z, y).
Axes of the slice: x: 2, y: 2, z: 4, core: 2. Of those that a mesh axis runs over, the one named last changes fastest.
Arguments:
- wavefield: bfloat16 [1024, 1024, 256], P('src', 'rcv'), may hold values from -6 to 6
- inverse_wavelet: float32 [2, 64], replicated, may hold values from -0.05 to 0.05
Outputs:
- primaries: bfloat16 [1024, 1024, 256], P('src', 'rcv')
All inputs are finite; a program needn't handle non-finite values.
Results may differ from a plain program's by a relative error of at most 0.0091.
Values may be sent and summed in bfloat16 or wider, within the bound.
No kernel may reach another device: no remote copies, remote signals or barrier semaphores. Data moves between devices by JAX's collectives and lax.ppermute only.
A program may use at most 256 MiB of HBM per device.

v0:
```python
import math
import jax
import jax.numpy as jnp
from jax import lax
from jax.sharding import PartitionSpec as P

F0 = 8


def tables(count_t, count_f, first):
    times = jnp.arange(count_t, dtype=jnp.int32)
    freqs = first + jnp.arange(count_f, dtype=jnp.int32)
    phase = freqs[:, None] * times[None, :] % count_t
    angle = phase.astype(jnp.float32) * (2.0 * math.pi / count_t)
    rows = jnp.stack([jnp.cos(angle), -jnp.sin(angle)], 1).reshape(2 * count_f, count_t)
    forward = (rows / math.sqrt(count_t)).astype(jnp.bfloat16)
    inverse = (rows / math.sqrt(count_f)).astype(jnp.bfloat16)
    return (forward, inverse)


def combine(mirror_real, mirror_imag, sq_real, sq_imag, cube_real, cube_imag, wave_real, wave_imag):
    two_real = wave_real * wave_real - wave_imag * wave_imag
    two_imag = 2.0 * wave_real * wave_imag
    out_real = (
        mirror_real
        - (wave_real * sq_real - wave_imag * sq_imag)
        + (two_real * cube_real - two_imag * cube_imag)
    )
    out_imag = (
        mirror_imag
        - (wave_real * sq_imag + wave_imag * sq_real)
        + (two_real * cube_imag + two_imag * cube_real)
    )
    return (out_real, out_imag)


def multiply(left_side, right_side):
    return jnp.einsum("fmk,fkn->fmn", left_side, right_side, preferred_element_type=jnp.float32)


def complex_product(left_side, right_side):
    real_part = multiply(left_side[:, 0], right_side[:, 0]) - multiply(
        left_side[:, 1], right_side[:, 1]
    )
    imag_part = multiply(left_side[:, 0], right_side[:, 1]) + multiply(
        left_side[:, 1], right_side[:, 0]
    )
    return (real_part, imag_part)


def local(wavefield, inverse_wavelet):
    src_rows, rcv_cols, samples = wavefield.shape
    count_f = inverse_wavelet.shape[1]
    groups = lax.axis_size("rcv")
    per_dev = count_f // groups
    forward, inverse = tables(samples, count_f, F0)
    spectra = jnp.einsum(
        "ct,srt->csr", forward, wavefield, preferred_element_type=jnp.float32
    ).astype(jnp.bfloat16)
    spectra = spectra.reshape(groups, 2 * per_dev, src_rows, rcv_cols)
    slices = lax.all_to_all(spectra, "rcv", split_axis=0, concat_axis=3, tiled=True)
    total_cols = slices.shape[3]
    slices = slices.reshape(per_dev, 2, src_rows, total_cols)
    whole = lax.all_gather(slices, "src", axis=2, tiled=True).astype(jnp.float32)
    all_rows = (0.5 * (whole + jnp.swapaxes(whole, 2, 3))).astype(jnp.bfloat16)
    mirrored = lax.dynamic_slice_in_dim(all_rows, lax.axis_index("src") * src_rows, src_rows, 2)
    sq_real, sq_imag = complex_product(mirrored, all_rows)
    squared = jnp.stack([sq_real, sq_imag], 1).astype(jnp.bfloat16)
    cube_real, cube_imag = complex_product(squared, all_rows)
    wavelet = lax.dynamic_slice_in_dim(inverse_wavelet, lax.axis_index("rcv") * per_dev, per_dev, 1)
    wave_real = wavelet[0][:, None, None]
    wave_imag = wavelet[1][:, None, None]
    out_real, out_imag = combine(
        mirrored[:, 0].astype(jnp.float32),
        mirrored[:, 1].astype(jnp.float32),
        sq_real,
        sq_imag,
        cube_real,
        cube_imag,
        wave_real,
        wave_imag,
    )
    cleaned = (
        jnp.stack([out_real, out_imag], 1)
        .astype(jnp.bfloat16)
        .reshape(1, 2 * per_dev, src_rows, total_cols)
    )
    returned = lax.all_to_all(cleaned, "rcv", split_axis=3, concat_axis=0, tiled=True)
    returned = returned.reshape(2 * count_f, src_rows, rcv_cols)
    return jnp.einsum("csr,ct->srt", returned, inverse, preferred_element_type=jnp.float32).astype(
        jnp.bfloat16
    )


def solution(mesh):
    placed = (P("src", "rcv", None), P())
    return jax.shard_map(
        local, mesh=mesh, in_specs=placed, out_specs=P("src", "rcv", None), check_vma=False
    )
```

profile of v0, /device:TPU:0, one launch (start us, length us, event | category | flops | bytes accessed | tf_op | source)
XLA Modules:
  0.0 942.9 jit_solution(6739649526145548966)
XLA Ops:
  6.5 0.3 fusion.25
  6.9 0.6 multiply_convert_fusion.1
  7.5 0.1 copy.29
  7.6 11.1 %convolution_convert_fusion.1 = bf16[128,256,128]{2,0,1:T(8,128)(2,1)} fusion(bf16[128,256,1]{1,0,2:T(8,128)(2,1)S(1)} %reshape.171, bf16[256,128,256]{2,1,0:T(8,128)(2,1)} %param.2), kind=kOutput, calls=%fused_computation.18 | convolution fusion | flops 2151677952 | bytes 25231360 | tf_op jit(solution)/shard_map/ct,srt->csr/dot_general | solution.py:57
  18.8 13.0 %copy.30 = bf16[8,16,256,128]{2,3,1,0:T(8,128)(2,1)} copy(bf16[8,16,256,128]{3,1,0,2:T(8,128)(2,1)} %bitcast.70) | data formatting | bytes 16777216 | tf_op jit(solution)/shard_map/reshape | solution.py:60
  31.7 190.4 %all_to_all.30 = bf16[8,16,256,128]{2,3,1,0:T(8,128)(2,1)} all-to-all(bf16[8,16,256,128]{2,3,1,0:T(8,128)(2,1)} %copy.30), channel_id=1, replica_groups=mesh['src'=4,'rcv'=8] {'rcv'}, dimensions={0} | all-to-all | bytes 16777216 | tf_op jit(solution)/shard_map/all_to_all | solution.py:61
  222.2 7.9 copy.31
  230.1 7.4 copy.32
  237.4 0.0 all-gather.2.cloned.1.call-update
  237.4 0.1 constant_dynamic-slice_fusion
  237.5 0.5 multiply_subtract_fusion
  238.1 0.6 slice_bitcast_fusion.15
  238.7 204.0 %all-gather.2.cloned.1.call-done = bf16[8,2,1024,1024]{2,3,0,1:T(8,128)(2,1)} async-done(((bf16[8,2,256,1024]{2,3,0,1:T(8,128)(2,1)}), bf16[8,2,1024,1024]{2,3,0,1:T(8,128)(2,1)}) %all-gather.2.cloned.1.call-update) | async-done | bytes 33554448 | tf_op jit(solution)/shard_map/all_gather | solution.py:64
  442.7 46.2 %copy.33 = f32[8,2,1024,1024]{3,2,0,1:T(8,128)} copy(bf16[8,2,1024,1024]{2,3,0,1:T(8,128)(2,1)} %all-gather.2.cloned.1.call-done) | data formatting | bytes 100663296 | tf_op jit(solution)/shard_map/convert_element_type | solution.py:64
  488.9 42.8 %fusion.1 = bf16[8,2,1024,1024]{3,2,0,1:T(8,128)(2,1)} fusion(f32[8,2,1024,1024]{3,2,0,1:T(8,128)} %copy.33, bf16[8,2,1024,1024]{2,3,0,1:T(8,128)(2,1)} %all-gather.2.cloned.1.call-done), kind=kLoop, calls=%fused_computation.2 | loop fusion | flops 67108864 | bytes 134217728 | tf_op jit(solution)/shard_map/convert_element_type | solution.py:65
  531.7 14.8 %fusion.5 = f32[8,256,1024]{2,1,0:T(8,128)} fusion(bf16[8,2,1024,1024]{3,2,0,1:T(8,128)(2,1)} %fusion.1, s32[]{:T(128)S(6)} %select_n.27), kind=kOutput, calls=%fused_computation.8 | convolution fusion | flops 4294967296 | bytes 29360132 | tf_op jit(solution)/shard_map/fmk,fkn->fmn/dot_general | solution.py:38
  546.5 15.0 %fusion.4 = f32[8,256,1024]{2,1,0:T(8,128)} fusion(bf16[8,2,1024,1024]{3,2,0,1:T(8,128)(2,1)} %fusion.1, s32[]{:T(128)S(6)} %add.70, s32[]{:T(128)S(6)} %select_n.27), kind=kOutput, calls=%fused_computation.7 | convolution fusion | flops 4294967296 | bytes 29360136 | tf_op jit(solution)/shard_map/fmk,fkn->fmn/dot_general | solution.py:38
  561.5 17.2 %fusion.13 = f32[8,256,1024]{2,1,0:T(8,128)} fusion(f32[8,256,1024]{2,1,0:T(8,128)} %fusion.5, bf16[8,2,1024,1024]{3,2,0,1:T(8,128)(2,1)} %fusion.1, s32[]{:T(128)S(6)} %add.70, s32[]{:T(128)S(6)} %select_n.27), kind=kOutput, calls=%fused_computation.23 | convolution fusion | flops 4297064448 | bytes 37748744 | tf_op jit(solution)/shard_map/fmk,fkn->fmn/dot_general | solution.py:38
  578.7 16.1 %fusion.6 = f32[8,256,1024]{2,1,0:T(8,128)} fusion(bf16[8,2,1024,1024]{3,2,0,1:T(8,128)(2,1)} %fusion.1, f32[8,256,1024]{2,1,0:T(8,128)} %fusion.13), kind=kOutput, calls=%fused_computation.9 | convolution fusion | flops 4297064448 | bytes 33554432 | tf_op jit(solution)/shard_map/fmk,fkn->fmn/dot_general | solution.py:38
  594.8 15.9 %fusion.3 = f32[8,256,1024]{2,1,0:T(8,128)} fusion(bf16[8,2,1024,1024]{3,2,0,1:T(8,128)(2,1)} %fusion.1, f32[8,256,1024]{2,1,0:T(8,128)} %fusion.13), kind=kOutput, calls=%fused_computation.6 | convolution fusion | flops 4297064448 | bytes 33554432 | tf_op jit(solution)/shard_map/fmk,fkn->fmn/dot_general | solution.py:38
  610.7 17.4 %fusion.14 = f32[8,256,1024]{2,1,0:T(8,128)} fusion(f32[8,256,1024]{2,1,0:T(8,128)} %fusion.4, bf16[8,2,1024,1024]{3,2,0,1:T(8,128)(2,1)} %fusion.1, s32[]{:T(128)S(6)} %select_n.27), kind=kOutput, calls=%fused_computation.24 | convolution fusion | flops 4297064448 | bytes 37748740 | tf_op jit(solution)/shard_map/fmk,fkn->fmn/dot_general | solution.py:38
  628.1 16.3 %fusion.2 = f32[8,256,1024]{2,1,0:T(8,128)} fusion(bf16[8,2,1024,1024]{3,2,0,1:T(8,128)(2,1)} %fusion.1, f32[8,256,1024]{2,1,0:T(8,128)} %fusion.14), kind=kOutput, calls=%fused_computation.5 | convolution fusion | flops 4297064448 | bytes 33554432 | tf_op jit(solution)/shard_map/fmk,fkn->fmn/dot_general | solution.py:38
  644.5 28.6 %fusion.11 = (bf16[8,1,256,1024]{3,2,0,1:T(8,128)(2,1)}, bf16[8,1,256,1024]{3,2,0,1:T(8,128)(2,1)}) fusion(f32[8,256,1024]{2,1,0:T(8,128)} %fusion.14, f32[8,256,1024]{2,1,0:T(8,128)} %fusion.13, f32[8]{0:T(128)S(1)} %copy-done.4, f32[8]{0:T(128)S(1)} %copy-done.3, f32[8]{0:T(128)S(1)} %copy-done.6, f32[8]{0:T(128)S(1)} %copy-done.5, ...), kind=kOutput, calls=%fused_computation.19 | convolution fusion | flops 4343201792 | bytes 83886216 | tf_op jit(solution)/shard_map/fmk,fkn->fmn/dot_general | solution.py:38
  673.1 7.6 pad_maximum_fusion
  680.7 8.0 copy.34
  688.7 12.5 %copy.35 = bf16[1,16,256,1024]{2,1,0,3:T(8,128)(2,1)} copy(bf16[1,16,256,1024]{3,2,1,0:T(8,128)(2,1)} %bitcast.73) | data formatting | bytes 16777216 | tf_op jit(solution)/shard_map/convert_element_type | solution.py:85
  701.1 5.6 all-to-all-start.1
  706.8 0.1 copy.38
  706.9 183.5 %all-to-all-done.1 = bf16[1,16,256,1024]{2,1,0,3:T(8,128)(2,1)} async-done(((bf16[1,16,256,1024]{2,1,0,3:T(8,128)(2,1)}), bf16[1,16,256,1024]{2,1,0,3:T(8,128)(2,1)}, u32[]{:S(2)}, u32[]{:S(2)}) %all-to-all-start.1) | async-done | bytes 8388640 | tf_op jit(solution)/shard_map/all_to_all | solution.py:88
  890.4 9.8 %copy.36 = bf16[1,16,256,1024]{2,3,1,0:T(8,128)(2,1)} copy(bf16[1,16,256,1024]{2,1,0,3:T(8,128)(2,1)} %all-to-all-done.1) | data formatting | bytes 16777216 | tf_op jit(solution)/shard_map/all_to_all | solution.py:88
  900.2 11.4 %copy.37 = bf16[8,1,16,256,128]{4,3,2,0,1:T(8,128)(2,1)} copy(bf16[8,1,16,256,128]{3,4,0,2,1:T(8,128)(2,1)} %bitcast.74) | data formatting | bytes 16777216 | tf_op jit(solution)/shard_map/all_to_all | solution.py:88
  911.6 24.2 %convolution_convert_fusion = bf16[256,128,256]{2,1,0:T(8,128)(2,1)} fusion(bf16[128,256,1]{1,0,2:T(8,128)(2,1)S(1)} %reshape.172, bf16[128,256,128]{2,1,0:T(8,128)(2,1)} %bitcast.71), kind=kOutput, calls=%fused_computation.13 | convolution fusion | flops 2155872256 | bytes 25231360 | tf_op jit(solution)/shard_map/csr,ct->srt/dot_general | solution.py:90
  (18 shorter events, 0.1 us)
Async XLA Ops:
  6.5 230.9 %copy-start = (f32[2,64]{1,0:T(2,128)S(1)}, f32[2,64]{1,0:T(2,128)}, u32[]{:S(2)}) copy-start(f32[2,64]{1,0:T(2,128)} %param.3) | copy-start | bytes 1540
  6.5 436.2 %all-gather.2.cloned.1.call-start = ((), (), s32[]{:S(2)}) async-start(), calls=%async_computation.2 | async-start | bytes 41943040 | tf_op jit(solution)/shard_map/all_gather | solution.py:64
  628.1 16.3 %copy-start.3 = (f32[8]{0:T(128)S(1)}, f32[8]{0:T(128)}, u32[]{:S(2)}) copy-start(f32[8]{0:T(128)} %get-tuple-element.11) | copy-start | bytes 100
  628.1 16.3 %copy-start.4 = (f32[8]{0:T(128)S(1)}, f32[8]{0:T(128)}, u32[]{:S(2)}) copy-start(f32[8]{0:T(128)} %get-tuple-element.12) | copy-start | bytes 100
  628.1 16.3 %copy-start.5 = (f32[8]{0:T(128)S(1)}, f32[8]{0:T(128)}, u32[]{:S(2)}) copy-start(f32[8]{0:T(128)} %get-tuple-element.9) | copy-start | bytes 100
  628.1 16.3 %copy-start.6 = (f32[8]{0:T(128)S(1)}, f32[8]{0:T(128)}, u32[]{:S(2)}) copy-start(f32[8]{0:T(128)} %get-tuple-element.10) | copy-start | bytes 100
  701.1 5.7 copy-start.2
  701.1 189.2 %all-to-all-start.1 = ((bf16[1,16,256,1024]{2,1,0,3:T(8,128)(2,1)}), bf16[1,16,256,1024]{2,1,0,3:T(8,128)(2,1)}, u32[]{:S(2)}, u32[]{:S(2)}) async-start(bf16[1,16,256,1024]{2,1,0,3:T(8,128)(2,1)} %copy.35), calls=%async_computation.1 | async-start | bytes 16777216 | tf_op jit(solution)/shard_map/all_to_all | solution.py:88
  911.6 24.3 %copy-start.1 = (f32[2,64]{1,0:T(2,128)S(1)}, f32[2,64]{1,0:T(2,128)}, u32[]{:S(2)}) copy-start(f32[2,64]{1,0:T(2,128)} %param.3) | copy-start | bytes 1540
Sparse Core Ops, SparseCore 0:
  237.6 205.0 all-gather.1
where the time goes:
time: 950 us; the launch traced here: 943 us
  waiting for transfers between devices  388 us (41%)
  blocking collectives  190 us (20%)
  matrix products  177 us (19%)
  local copies, waits for them, and re-layouts  117 us (12%)
  other arithmetic  52 us (5%)
  between operations  13.7 us (1%)
    all_gather x1, waiting for transfers between devices, local(): lax.all_gather(slices, 'src', axis=2, tiled=True).astype(jnp.float32)  204 us
    all_to_all x1, blocking collectives, local(): lax.all_to_all(spectra, 'rcv', split_axis=0, concat_axis=3, tiled=True)  190 us
    all_to_all x1, waiting for transfers between devices, local(): lax.all_to_all(cleaned, 'rcv', split_axis=3, concat_axis=0, tiled=True)  183 us
    dot_general x8, matrix products, multiply(): jnp.einsum('fmk,fkn->fmn', left_side, right_side, preferred_element_type=...  141 us
    convert_element_type x1, local copies, waits for them, and re-layouts, local(): lax.all_gather(slices, 'src', axis=2, tiled=True).astype(jnp.float32)  46.2 us
    convert_element_type x1, other arithmetic, local(): all_rows = (0.5 * (whole + jnp.swapaxes(whole, 2, 3))).astype(jnp.bfloat16)  42.8 us
    dot_general x1, matrix products, local(): jnp.einsum('csr,ct->srt', returned, inverse, preferred_element_type=jnp.f...  24.2 us
    all_to_all x2, local copies, waits for them, and re-layouts, local(): lax.all_to_all(cleaned, 'rcv', split_axis=3, concat_axis=0, tiled=True)  21.2 us
  transfers between devices with their start and end apart: 2, of which 2 were waited for; matrix products, arithmetic and copies ran while one was open for 0% of the time, Pallas kernels for 0%

commit v1 on v0

--- a/solution.py
+++ b/solution.py
@@ -5,6 +5,18 @@
 from jax.sharding import PartitionSpec as P
 
 F0 = 8
+
+
+def rotated_exchange(value, axis, split, join):
+    ways, here = (lax.axis_size(axis), lax.axis_index(axis))
+    width = value.shape[split] // ways
+    turned = jnp.roll(value, -here * width, axis=split)
+    got = [lax.slice_in_dim(turned, 0, width, axis=split)]
+    for far in range(1, ways):
+        sent = lax.slice_in_dim(turned, far * width, (far + 1) * width, axis=split)
+        got.append(lax.ppermute(sent, axis, [(d, (d + far) % ways) for d in range(ways)]))
+    line = jnp.concatenate(got[::-1], axis=join)
+    return jnp.roll(line, (here + 1) * got[0].shape[join], axis=join)
 
 
 def tables(count_t, count_f, first):
@@ -58,7 +70,7 @@
         "ct,srt->csr", forward, wavefield, preferred_element_type=jnp.float32
     ).astype(jnp.bfloat16)
     spectra = spectra.reshape(groups, 2 * per_dev, src_rows, rcv_cols)
-    slices = lax.all_to_all(spectra, "rcv", split_axis=0, concat_axis=3, tiled=True)
+    slices = rotated_exchange(spectra, "rcv", 0, 3)
     total_cols = slices.shape[3]
     slices = slices.reshape(per_dev, 2, src_rows, total_cols)
     whole = lax.all_gather(slices, "src", axis=2, tiled=True).astype(jnp.float32)

time: 950 us -> 996 us (1.048)
  blocking collectives: 190 us -> 0 us
  waiting for transfers between devices: 388 us -> 559 us
  local copies, waits for them, and re-layouts: 117 us -> 155 us
    all_to_all x1 -> x0, blocking collectives: 190 us -> none  [local(): lax.all_to_all(spectra, 'rcv', split_axis=0, concat_axis=3, tiled=True)]
    ppermute x0 -> x7, waiting for transfers between devices: none -> 173 us  [rotated_exchange(): lax.ppermute(sent, axis, [(d, (d + far) % ways) for d in range(ways)])]
    unnamed x14 -> x31, local copies, waits for them, and re-layouts: 0.03 us -> 30.2 us
  transfers between devices with their start and end apart: 2 -> 9, of which waited for: 2 -> 6; matrix products, arithmetic and copies ran while one was open for 0% -> 1% of each run, Pallas kernels for 0% -> 0%
where the time goes in v1:
time: 996 us; the launch traced here: 986 us
  waiting for transfers between devices  559 us (56%)
  matrix products  185 us (19%)
  local copies, waits for them, and re-layouts  155 us (16%)
  other arithmetic  57.5 us (6%)
  starting transfers between devices  15.4 us (2%)
  between operations  14 us (1%)
    all_gather x1, waiting for transfers between devices, local(): lax.all_gather(slices, 'src', axis=2, tiled=True).astype(jnp.float32)  202 us
    all_to_all x1, waiting for transfers between devices, local(): lax.all_to_all(cleaned, 'rcv', split_axis=3, concat_axis=0, tiled=True)  183 us
    ppermute x7, waiting for transfers between devices, rotated_exchange(): lax.ppermute(sent, axis, [(d, (d + far) % ways) for d in range(ways)])  173 us
    dot_general x8, matrix products, multiply(): jnp.einsum('fmk,fkn->fmn', left_side, right_side, preferred_element_type=...  150 us
    convert_element_type x1, local copies, waits for them, and re-layouts, local(): lax.all_gather(slices, 'src', axis=2, tiled=True).astype(jnp.float32)  46.3 us
    convert_element_type x1, other arithmetic, local(): all_rows = (0.5 * (whole + jnp.swapaxes(whole, 2, 3))).astype(jnp.bfloat16)  42.7 us
    unnamed x31, local copies, waits for them, and re-layouts  30.2 us
    dot_general x1, matrix products, local(): jnp.einsum('csr,ct->srt', returned, inverse, preferred_element_type=jnp.f...  24.3 us
  transfers between devices with their start and end apart: 9, of which 6 were waited for; matrix products, arithmetic and copies ran while one was open for 1% of the time, Pallas kernels for 0%

profile of v1, /device:TPU:0, one launch (start us, length us, event | category | flops | bytes accessed | tf_op | source)
XLA Modules:
  0.0 985.9 jit_solution(1199431623306373723)
XLA Ops:
  7.6 11.1 %convolution_convert_fusion.1 = bf16[128,256,128]{2,0,1:T(8,128)(2,1)} fusion(bf16[128,256,1]{1,0,2:T(8,128)(2,1)S(1)} %reshape.170, bf16[256,128,256]{2,1,0:T(8,128)(2,1)} %param.2), kind=kOutput, calls=%fused_computation.21 | convolution fusion | flops 2151677952 | bytes 25231360 | tf_op jit(solution)/shard_map/ct,srt->csr/dot_general | solution.py:69
  18.8 12.0 %copy.31 = bf16[8,16,256,128]{3,2,1,0:T(8,128)(2,1)} copy(bf16[8,16,256,128]{3,1,0,2:T(8,128)(2,1)} %bitcast.66) | data formatting | bytes 16777216 | tf_op jit(solution)/shard_map/reshape | solution.py:72
  30.8 5.6 fusion.10
  36.5 3.3 copy-done.2
  39.7 2.4 fusion.31
  42.1 6.0 collective-permute-start
  48.6 3.0 collective-permute-start.3
  51.6 20.1 %collective-permute-done = bf16[1,16,256,128]{3,2,1,0:T(8,128)(2,1)S(1)} collective-permute-done((bf16[1,16,256,128]{3,2,1,0:T(8,128)(2,1)S(1)}, bf16[1,16,256,128]{3,2,1,0:T(8,128)(2,1)S(1)}, u32[]{:S(2)}, u32[]{:S(2)}) %collective-permute-start) | collective-permute-done | bytes 1048608 | tf_op jit(solution)/shard_map/ppermute | solution.py:17
  71.7 22.5 %collective-permute-done.1 = bf16[1,16,256,128]{3,2,1,0:T(8,128)(2,1)S(1)} collective-permute-done((bf16[1,16,256,128]{3,2,1,0:T(8,128)(2,1)S(1)}, bf16[1,16,256,128]{3,2,1,0:T(8,128)(2,1)S(1)}, u32[]{:S(2)}, u32[]{:S(2)}) %collective-permute-start.1) | collective-permute-done | bytes 1048608 | tf_op jit(solution)/shard_map/ppermute | solution.py:17
  96.6 20.3 %collective-permute-done.2 = bf16[1,16,256,128]{3,2,1,0:T(8,128)(2,1)S(1)} collective-permute-done((bf16[1,16,256,128]{3,2,1,0:T(8,128)(2,1)}, bf16[1,16,256,128]{3,2,1,0:T(8,128)(2,1)S(1)}, u32[]{:S(2)}, u32[]{:S(2)}) %collective-permute-start.2) | collective-permute-done | bytes 1048608 | tf_op jit(solution)/shard_map/ppermute | solution.py:17
  117.9 110.0 %collective-permute-done.3 = bf16[1,16,256,128]{3,2,1,0:T(8,128)(2,1)} collective-permute-done((bf16[1,16,256,128]{3,2,1,0:T(8,128)(2,1)}, bf16[1,16,256,128]{3,2,1,0:T(8,128)(2,1)}, u32[]{:S(2)}, u32[]{:S(2)}) %collective-permute-start.3) | collective-permute-done | bytes 1048608 | tf_op jit(solution)/shard_map/ppermute | solution.py:17
  253.9 8.0 constant_dynamic-slice_fusion.1
  261.9 11.7 %copy.33 = bf16[8,2,256,1024]{2,3,0,1:T(8,128)(2,1)} copy(bf16[8,2,256,1024]{3,2,1,0:T(8,128)(2,1)} %bitcast.68) | data formatting | bytes 16777216 | tf_op jit(solution)/shard_map/reshape | solution.py:75
  274.9 202.1 %all-gather.2.cloned.1.call-done = bf16[8,2,1024,1024]{2,3,0,1:T(8,128)(2,1)} async-done(((bf16[8,2,256,1024]{2,3,0,1:T(8,128)(2,1)}), bf16[8,2,1024,1024]{2,3,0,1:T(8,128)(2,1)}) %all-gather.2.cloned.1.call-update) | async-done | bytes 33554448 | tf_op jit(solution)/shard_map/all_gather | solution.py:76
  477.0 46.3 %copy.34 = f32[8,2,1024,1024]{3,2,0,1:T(8,128)} copy(bf16[8,2,1024,1024]{2,3,0,1:T(8,128)(2,1)} %all-gather.2.cloned.1.call-done) | data formatting | bytes 100663296 | tf_op jit(solution)/shard_map/convert_element_type | solution.py:76
  523.3 42.7 %fusion.1 = bf16[8,2,1024,1024]{3,2,0,1:T(8,128)(2,1)} fusion(f32[8,2,1024,1024]{3,2,0,1:T(8,128)} %copy.34, bf16[8,2,1024,1024]{2,3,0,1:T(8,128)(2,1)} %all-gather.2.cloned.1.call-done), kind=kLoop, calls=%fused_computation.2 | loop fusion | flops 67108864 | bytes 134217728 | tf_op jit(solution)/shard_map/convert_element_type | solution.py:77
  566.0 14.8 %fusion.5 = f32[8,256,1024]{2,1,0:T(8,128)} fusion(bf16[8,2,1024,1024]{3,2,0,1:T(8,128)(2,1)} %fusion.1, s32[]{:T(128)S(6)} %select_n.53), kind=kOutput, calls=%fused_computation.10 | convolution fusion | flops 4294967296 | bytes 29360132 | tf_op jit(solution)/shard_map/fmk,fkn->fmn/dot_general | solution.py:50
  580.8 15.0 %fusion.4 = f32[8,256,1024]{2,1,0:T(8,128)} fusion(bf16[8,2,1024,1024]{3,2,0,1:T(8,128)(2,1)} %fusion.1, s32[]{:T(128)S(6)} %add.97, s32[]{:T(128)S(6)} %select_n.53), kind=kOutput, calls=%fused_computation.9 | convolution fusion | flops 4294967296 | bytes 29360136 | tf_op jit(solution)/shard_map/fmk,fkn->fmn/dot_general | solution.py:50
  595.8 17.2 %fusion.14 = f32[8,256,1024]{2,1,0:T(8,128)} fusion(f32[8,256,1024]{2,1,0:T(8,128)} %fusion.5, bf16[8,2,1024,1024]{3,2,0,1:T(8,128)(2,1)} %fusion.1, s32[]{:T(128)S(6)} %add.97, s32[]{:T(128)S(6)} %select_n.53), kind=kOutput, calls=%fused_computation.26 | convolution fusion | flops 4297064448 | bytes 37748744 | tf_op jit(solution)/shard_map/fmk,fkn->fmn/dot_general | solution.py:50
  613.0 24.7 %fusion.6 = f32[8,256,1024]{2,1,0:T(8,128)} fusion(bf16[8,2,1024,1024]{3,2,0,1:T(8,128)(2,1)} %fusion.1, f32[8,256,1024]{2,1,0:T(8,128)} %fusion.14), kind=kOutput, calls=%fused_computation.11 | convolution fusion | flops 4297064448 | bytes 33554432 | tf_op jit(solution)/shard_map/fmk,fkn->fmn/dot_general | solution.py:50
  637.7 15.9 %fusion.3 = f32[8,256,1024]{2,1,0:T(8,128)} fusion(bf16[8,2,1024,1024]{3,2,0,1:T(8,128)(2,1)} %fusion.1, f32[8,256,1024]{2,1,0:T(8,128)} %fusion.14), kind=kOutput, calls=%fused_computation.8 | convolution fusion | flops 4297064448 | bytes 33554432 | tf_op jit(solution)/shard_map/fmk,fkn->fmn/dot_general | solution.py:50
  653.6 17.4 %fusion.15 = f32[8,256,1024]{2,1,0:T(8,128)} fusion(f32[8,256,1024]{2,1,0:T(8,128)} %fusion.4, bf16[8,2,1024,1024]{3,2,0,1:T(8,128)(2,1)} %fusion.1, s32[]{:T(128)S(6)} %select_n.53), kind=kOutput, calls=%fused_computation.27 | convolution fusion | flops 4297064448 | bytes 37748740 | tf_op jit(solution)/shard_map/fmk,fkn->fmn/dot_general | solution.py:50
  671.0 16.1 %fusion.2 = f32[8,256,1024]{2,1,0:T(8,128)} fusion(bf16[8,2,1024,1024]{3,2,0,1:T(8,128)(2,1)} %fusion.1, f32[8,256,1024]{2,1,0:T(8,128)} %fusion.15), kind=kOutput, calls=%fused_computation.7 | convolution fusion | flops 4297064448 | bytes 33554432 | tf_op jit(solution)/shard_map/fmk,fkn->fmn/dot_general | solution.py:50
  687.2 28.6 %fusion.12 = (bf16[8,1,256,1024]{3,2,0,1:T(8,128)(2,1)}, bf16[8,1,256,1024]{3,2,0,1:T(8,128)(2,1)}) fusion(f32[8,256,1024]{2,1,0:T(8,128)} %fusion.15, f32[8,256,1024]{2,1,0:T(8,128)} %fusion.14, f32[8]{0:T(128)S(1)} %copy-done.5, f32[8]{0:T(128)S(1)} %copy-done.4, f32[8]{0:T(128)S(1)} %copy-done.7, f32[8]{0:T(128)S(1)} %copy-done.6, ...), kind=kOutput, calls=%fused_computation.22 | convolution fusion | flops 4343201792 | bytes 83886216 | tf_op jit(solution)/shard_map/fmk,fkn->fmn/dot_general | solution.py:50
  715.8 7.6 pad_maximum_fusion
  723.4 8.0 copy.35
  731.4 12.5 %copy.36 = bf16[1,16,256,1024]{2,1,0,3:T(8,128)(2,1)} copy(bf16[1,16,256,1024]{3,2,1,0:T(8,128)(2,1)} %bitcast.69) | data formatting | bytes 16777216 | tf_op jit(solution)/shard_map/convert_element_type | solution.py:97
  743.9 5.6 all-to-all-start
  749.6 183.5 %all-to-all-done = bf16[1,16,256,1024]{2,1,0,3:T(8,128)(2,1)} async-done(((bf16[1,16,256,1024]{2,1,0,3:T(8,128)(2,1)}), bf16[1,16,256,1024]{2,1,0,3:T(8,128)(2,1)}, u32[]{:S(2)}, u32[]{:S(2)}) %all-to-all-start) | async-done | bytes 8388640 | tf_op jit(solution)/shard_map/all_to_all | solution.py:100
  933.1 9.8 copy.37
  942.9 11.4 %copy.38 = bf16[8,1,16,256,128]{4,3,2,0,1:T(8,128)(2,1)} copy(bf16[8,1,16,256,128]{3,4,0,2,1:T(8,128)(2,1)} %bitcast.70) | data formatting | bytes 16777216 | tf_op jit(solution)/shard_map/all_to_all | solution.py:100
  954.3 24.3 %convolution_convert_fusion = bf16[256,128,256]{2,1,0:T(8,128)(2,1)} fusion(bf16[128,256,1]{1,0,2:T(8,128)(2,1)S(1)} %reshape.171, bf16[128,256,128]{2,1,0:T(8,128)(2,1)} %bitcast.67), kind=kOutput, calls=%fused_computation.15 | convolution fusion | flops 2155872256 | bytes 25231360 | tf_op jit(solution)/shard_map/csr,ct->srt/dot_general | solution.py:102
  (51 shorter events, 32.4 us)
Async XLA Ops:
  6.5 267.1 %copy-start = (f32[2,64]{1,0:T(2,128)S(1)}, f32[2,64]{1,0:T(2,128)}, u32[]{:S(2)}) copy-start(f32[2,64]{1,0:T(2,128)} %param.3) | copy-start | bytes 1540
  6.5 470.5 %all-gather.2.cloned.1.call-start = ((), (), s32[]{:S(2)}) async-start(), calls=%async_computation.1 | async-start | bytes 41943040 | tf_op jit(solution)/shard_map/all_gather | solution.py:76
  36.5 3.3 copy-start.2
  42.1 29.6 %collective-permute-start = (bf16[1,16,256,128]{3,2,1,0:T(8,128)(2,1)S(1)}, bf16[1,16,256,128]{3,2,1,0:T(8,128)(2,1)S(1)}, u32[]{:S(2)}, u32[]{:S(2)}) collective-permute-start(bf16[1,16,256,128]{3,2,1,0:T(8,128)(2,1)S(1)} %get-tuple-element.13), channel_id=1, source_target_pairs={{0,7},{1,0},{2,1},{3,2},{4,3},{5,4},{6,5},{7,6},{8,15},{9,8},{10,9... | collective-permute-start | bytes 3145736 | tf_op jit(solution)/shard_map/ppermute | solution.py:17
  48.1 46.1 %collective-permute-start.1 = (bf16[1,16,256,128]{3,2,1,0:T(8,128)(2,1)S(1)}, bf16[1,16,256,128]{3,2,1,0:T(8,128)(2,1)S(1)}, u32[]{:S(2)}, u32[]{:S(2)}) collective-permute-start(bf16[1,16,256,128]{3,2,1,0:T(8,128)(2,1)S(1)} %get-tuple-element.12), channel_id=1, source_target_pairs={{0,6},{1,7},{2,0},{3,1},{4,2},{5,3},{6,4},{7,5},{8,14},{9,15},{10,... | collective-permute-start | bytes 3145736 | tf_op jit(solution)/shard_map/ppermute | solution.py:17
  48.6 68.2 %collective-permute-start.2 = (bf16[1,16,256,128]{3,2,1,0:T(8,128)(2,1)}, bf16[1,16,256,128]{3,2,1,0:T(8,128)(2,1)S(1)}, u32[]{:S(2)}, u32[]{:S(2)}) collective-permute-start(bf16[1,16,256,128]{3,2,1,0:T(8,128)(2,1)} %get-tuple-element.11), channel_id=1, source_target_pairs={{0,5},{1,6},{2,7},{3,0},{4,1},{5,2},{6,3},{7,4},{8,13},{9,14},{10,... | collective-permute-start | bytes 3145736 | tf_op jit(solution)/shard_map/ppermute | solution.py:17
  48.6 179.3 %collective-permute-start.3 = (bf16[1,16,256,128]{3,2,1,0:T(8,128)(2,1)}, bf16[1,16,256,128]{3,2,1,0:T(8,128)(2,1)}, u32[]{:S(2)}, u32[]{:S(2)}) collective-permute-start(bf16[1,16,256,128]{3,2,1,0:T(8,128)(2,1)} %get-tuple-element.10), channel_id=1, source_target_pairs={{0,4},{1,5},{2,6},{3,7},{4,0},{5,1},{6,2},{7,3},{8,12},{9,13},{10,... | collective-permute-start | bytes 3145736 | tf_op jit(solution)/shard_map/ppermute | solution.py:17
  51.6 178.6 %collective-permute-start.4 = (bf16[1,16,256,128]{3,2,1,0:T(8,128)(2,1)}, bf16[1,16,256,128]{3,2,1,0:T(8,128)(2,1)}, u32[]{:S(2)}, u32[]{:S(2)}) collective-permute-start(bf16[1,16,256,128]{3,2,1,0:T(8,128)(2,1)} %get-tuple-element.9), channel_id=1, source_target_pairs={{0,3},{1,4},{2,5},{3,6},{4,7},{5,0},{6,1},{7,2},{8,11},{9,12},{10,... | collective-permute-start | bytes 3145736 | tf_op jit(solution)/shard_map/ppermute | solution.py:17
  71.7 160.7 %collective-permute-start.5 = (bf16[1,16,256,128]{3,2,1,0:T(8,128)(2,1)}, bf16[1,16,256,128]{3,2,1,0:T(8,128)(2,1)}, u32[]{:S(2)}, u32[]{:S(2)}) collective-permute-start(bf16[1,16,256,128]{3,2,1,0:T(8,128)(2,1)} %get-tuple-element.8), channel_id=1, source_target_pairs={{0,2},{1,3},{2,4},{3,5},{4,6},{5,7},{6,0},{7,1},{8,10},{9,11},{10,... | collective-permute-start | bytes 3145736 | tf_op jit(solution)/shard_map/ppermute | solution.py:17
  94.2 140.6 %collective-permute-start.6 = (bf16[1,16,256,128]{3,2,1,0:T(8,128)(2,1)}, bf16[1,16,256,128]{3,2,1,0:T(8,128)(2,1)}, u32[]{:S(2)}, u32[]{:S(2)}) collective-permute-start(bf16[1,16,256,128]{3,2,1,0:T(8,128)(2,1)} %get-tuple-element.7), channel_id=1, source_target_pairs={{0,1},{1,2},{2,3},{3,4},{4,5},{5,6},{6,7},{7,0},{8,9},{9,10},{10,1... | collective-permute-start | bytes 3145736 | tf_op jit(solution)/shard_map/ppermute | solution.py:17
  671.0 16.1 %copy-start.4 = (f32[8]{0:T(128)S(1)}, f32[8]{0:T(128)}, u32[]{:S(2)}) copy-start(f32[8]{0:T(128)} %get-tuple-element.18) | copy-start | bytes 100
  671.0 16.1 %copy-start.5 = (f32[8]{0:T(128)S(1)}, f32[8]{0:T(128)}, u32[]{:S(2)}) copy-start(f32[8]{0:T(128)} %get-tuple-element.19) | copy-start | bytes 100
  671.0 16.1 %copy-start.6 = (f32[8]{0:T(128)S(1)}, f32[8]{0:T(128)}, u32[]{:S(2)}) copy-start(f32[8]{0:T(128)} %get-tuple-element.16) | copy-start | bytes 100
  671.0 16.1 %copy-start.7 = (f32[8]{0:T(128)S(1)}, f32[8]{0:T(128)}, u32[]{:S(2)}) copy-start(f32[8]{0:T(128)} %get-tuple-element.17) | copy-start | bytes 100
  743.9 5.7 copy-start.3
  743.9 189.2 %all-to-all-start = ((bf16[1,16,256,1024]{2,1,0,3:T(8,128)(2,1)}), bf16[1,16,256,1024]{2,1,0,3:T(8,128)(2,1)}, u32[]{:S(2)}, u32[]{:S(2)}) async-start(bf16[1,16,256,1024]{2,1,0,3:T(8,128)(2,1)} %copy.36), calls=%async_computation | async-start | bytes 16777216 | tf_op jit(solution)/shard_map/all_to_all | solution.py:100
  954.3 24.3 %copy-start.1 = (f32[2,64]{1,0:T(2,128)S(1)}, f32[2,64]{1,0:T(2,128)}, u32[]{:S(2)}) copy-start(f32[2,64]{1,0:T(2,128)} %param.3) | copy-start | bytes 1540
Sparse Core Ops, SparseCore 0:
  273.8 203.2 all-gather.1
